TPU v7x, 32 devices: a whole 2x2x4 slice. The times are simulated.
32 devices in a mesh: ctx: 8 (over y, x, core), tp: 4 (over z).
Axes of the slice: x: 2, y: 2, z: 4, core: 2. Of those that a mesh axis runs over, the one named last changes fastest.
Arguments:
- inputs: bfloat16 [4096, 2048], P(('ctx', 'tp')), may hold values from -54 to 54
- norm_gain: float32 [2048], replicated, may hold values from 0.1 to 1.9
- qkv_weight: bfloat16 [2048, 3, 2048], P(None, None, 'tp'), may hold values from -0.125 to 0.125
- head_gain: float32 [2048], P('tp'), may hold values from 0.1 to 1.9
- out_weight: bfloat16 [2048, 2048], P('tp'), may hold values from -0.125 to 0.125
- out_cotangent: bfloat16 [4096, 2048], P(('ctx', 'tp')), may hold values from -6 to 6
Outputs:
- outputs: bfloat16 [4096, 2048], P(('ctx', 'tp'))
- input_grad: bfloat16 [4096, 2048], P(('ctx', 'tp'))
- qkv_grad: float32 [2048, 3, 2048], P('ctx', None, 'tp')
- out_grad_t: float32 [2048, 2048], P('ctx', 'tp')
All inputs are finite; a program needn't handle non-finite values.
Results may differ from a plain program's by a relative error of at most 0.015.
The roundings to bfloat16 on the way count: a program that leaves them out, or rounds other values in their place, can miss the bound.
Values may be sent and summed in bfloat16 or wider, within the bound.
A program may use at most 128 MiB of HBM per device.

v0:
```python
import math
import jax
import jax.numpy as jnp
from jax import lax
from jax.sharding import PartitionSpec as P

DH = 128
EPSILON = 1e-05
highest = lax.Precision.HIGHEST


def carried_in(array, axis, combine, identity, reverse):
    devices, place = (lax.axis_size(axis), lax.axis_index(axis))
    everything = lax.all_gather(array.astype(jnp.bfloat16), axis)
    start = jnp.broadcast_to(jnp.asarray(identity, array.dtype), array.shape)

    def hop(k, before):
        at = devices - 1 - k if reverse else k
        reached = at > place if reverse else at < place
        new = combine(before, everything[at].astype(array.dtype))
        return jnp.where(reached, new, before)

    return lax.fori_loop(0, devices, hop, start)


def row_scale(rows):
    return lax.rsqrt(jnp.mean(rows * rows, axis=-1, keepdims=True) + EPSILON)


def add_states(earlier, later):
    return earlier + later


def shards(inputs, norm_gain, qkv_weight, head_gain, out_weight, out_cotangent):
    width = inputs.shape[1]
    local_width = qkv_weight.shape[2]
    heads = local_width // DH
    own_rows = inputs.shape[0]
    block = own_rows * lax.axis_size("tp")
    total_tokens = block * lax.axis_size("ctx")
    factor = 1.0 / math.sqrt(total_tokens)
    ctx_rows = width // lax.axis_size("ctx")
    flat_weight = qkv_weight.reshape(width, 3 * local_width)
    piece_f = lax.all_gather(inputs, "tp", axis=0, tiled=True).astype(jnp.float32)
    normed_rows = (piece_f * row_scale(piece_f) * norm_gain).astype(jnp.bfloat16)
    projected_rows = jnp.dot(normed_rows, flat_weight, preferred_element_type=jnp.float32).astype(
        jnp.bfloat16
    )
    joined = jnp.concatenate([normed_rows, projected_rows], axis=1)
    normed = joined[:, :width]
    projected = joined[:, width:].reshape(block, 3, heads, DH)
    queries = projected[:, 0]
    key_rows = projected[:, 1]
    values = projected[:, 2]
    local_states = jnp.einsum("shd,she->hde", key_rows, values, preferred_element_type=jnp.float32)
    empty_states = jnp.zeros_like(local_states)
    states = carried_in(local_states, "ctx", add_states, empty_states, False)
    causal = jnp.arange(block)[:, None] >= jnp.arange(block)[None, :]
    raw_scores = jnp.einsum("thd,shd->hts", queries, key_rows, preferred_element_type=jnp.float32)
    scores = jnp.where(causal[None], raw_scores, 0.0).astype(jnp.bfloat16)
    local_part = jnp.einsum("hts,she->the", scores, values, preferred_element_type=jnp.float32)
    carried = jnp.einsum("thd,hde->the", queries.astype(jnp.float32), states, precision=highest)
    attended = local_part + carried
    scale_head = row_scale(attended)
    gains = head_gain.reshape(heads, DH)
    mixed = (attended * scale_head * gains).astype(jnp.bfloat16).reshape(block, local_width)
    rows = mixed
    attn_sum = lax.psum_scatter(
        jnp.dot(rows, out_weight, preferred_element_type=jnp.float32).astype(jnp.bfloat16),
        "tp",
        scatter_dimension=0,
        tiled=True,
    ).astype(jnp.float32)
    inputs_f = inputs.astype(jnp.float32)
    outputs = (inputs_f + attn_sum).astype(jnp.bfloat16)
    cotangent = lax.all_gather(out_cotangent, "tp", axis=0, tiled=True)
    grad_mixed = lax.dot_general(
        cotangent, out_weight, (((1,), (1,)), ((), ())), preferred_element_type=jnp.float32
    ).reshape(block, heads, DH)
    weighted = grad_mixed * gains
    cube_head = scale_head * scale_head * scale_head
    grad_attended = (
        scale_head * weighted
        - cube_head * attended * jnp.mean(weighted * attended, axis=-1, keepdims=True)
    ).astype(jnp.bfloat16)
    local_grads = jnp.einsum(
        "thd,the->hde", queries, grad_attended, preferred_element_type=jnp.float32
    )
    columns = cotangent
    out_grad_t = lax.psum_scatter(
        (
            lax.dot_general(
                columns, mixed, (((0,), (0,)), ((), ())), preferred_element_type=jnp.float32
            )
            * factor
        ).astype(jnp.bfloat16),
        "ctx",
        scatter_dimension=0,
        tiled=True,
    ).astype(jnp.float32)
    raw_grad = jnp.einsum("the,she->hts", grad_attended, values, preferred_element_type=jnp.float32)
    grad_scores = jnp.where(causal[None], raw_grad, 0.0).astype(jnp.bfloat16)
    grad_query = (
        jnp.einsum("hts,shd->thd", grad_scores, key_rows, preferred_element_type=jnp.float32)
        + jnp.einsum("the,hde->thd", grad_attended.astype(jnp.float32), states, precision=highest)
    ).astype(jnp.bfloat16)
    grad_states = carried_in(local_grads, "ctx", add_states, empty_states, True)
    grad_key = jnp.einsum(
        "hts,thd->shd", grad_scores, queries, preferred_element_type=jnp.float32
    ) + jnp.einsum("she,hde->shd", values.astype(jnp.float32), grad_states, precision=highest)
    grad_value = jnp.einsum(
        "hts,the->she", scores, grad_attended, preferred_element_type=jnp.float32
    ) + jnp.einsum("shd,hde->she", key_rows.astype(jnp.float32), grad_states, precision=highest)
    grad_key, grad_value = (grad_key.astype(jnp.bfloat16), grad_value.astype(jnp.bfloat16))
    grad_proj = jnp.stack([grad_query, grad_key, grad_value], axis=1).reshape(
        block, 3 * local_width
    )
    columns = normed
    product = lax.dot_general(
        columns, grad_proj, (((0,), (0,)), ((), ())), preferred_element_type=jnp.float32
    )
    qkv_grad = lax.psum_scatter(
        (product * factor)
        .reshape(ctx_rows * lax.axis_size("ctx"), 3, local_width)
        .astype(jnp.bfloat16),
        "ctx",
        scatter_dimension=0,
        tiled=True,
    ).astype(jnp.float32)
    rows = grad_proj
    grad_normed = lax.psum_scatter(
        lax.dot_general(
            rows, flat_weight, (((1,), (1,)), ((), ())), preferred_element_type=jnp.float32
        ).astype(jnp.bfloat16),
        "tp",
        scatter_dimension=0,
        tiled=True,
    ).astype(jnp.float32)
    scale_in = row_scale(inputs_f)
    weighted_in = grad_normed * norm_gain
    cube_in = scale_in * scale_in * scale_in
    input_grad = (
        out_cotangent.astype(jnp.float32)
        + scale_in * weighted_in
        - cube_in * inputs_f * jnp.mean(weighted_in * inputs_f, axis=-1, keepdims=True)
    ).astype(jnp.bfloat16)
    return (outputs, input_grad, qkv_grad, out_grad_t)


def solution(mesh):
    in_specs = (
        P(("ctx", "tp"), None),
        P(),
        P(None, None, "tp"),
        P("tp"),
        P("tp", None),
        P(("ctx", "tp"), None),
    )
    out_specs = (
        P(("ctx", "tp"), None),
        P(("ctx", "tp"), None),
        P("ctx", None, "tp"),
        P("ctx", "tp"),
    )
    return jax.shard_map(shards, mesh=mesh, in_specs=in_specs, out_specs=out_specs, check_vma=False)
```

profile of v0, /device:TPU:0, one launch (start us, length us, event | category | flops | bytes accessed | tf_op | source)
XLA Modules:
  0.0 377.1 jit_solution(10722562484087680778)
XLA Ops:
  8.7 8.8 %copy.45 = bf16[2048,3,512]{0,2,1:T(8,128)(2,1)} copy(bf16[2048,3,512]{2,0,1:T(8,128)(2,1)} %param.12) | data formatting | bytes 12582912 | tf_op args[2]
  17.6 40.7 %all-gather.7.cloned.1.call-done = bf16[512,2048]{1,0:T(8,128)(2,1)} async-done(((bf16[128,2048]{1,0:T(8,128)(2,1)}), bf16[512,2048]{1,0:T(8,128)(2,1)}) %all-gather.7.cloned.1.call-update) | async-done | bytes 2097168 | tf_op jit(solution)/shard_map/all_gather | solution.py:44
  60.5 7.6 %convolution_convert_fusion.2 = bf16[512,1536]{1,0:T(8,128)(2,1)} fusion(bf16[2048,1536]{0,1:T(8,128)(2,1)} %bitcast.80, bf16[512,2048]{1,0:T(8,128)(2,1)S(1)} %copy-done.12, f32[2048]{0:T(1024)S(1)} %copy-done.19, f32[512]{0:T(512)S(1)} %add_rsqrt_fusion.1), kind=kOutput, calls=%fused_computation.13 | convolution fusion | flops 3226206208 | bytes 9971712 | tf_op jit(solution)/shard_map/dot_general | solution.py:46
  68.1 3.9 %reshape.88 = bf16[512,3,4,128]{3,2,1,0:T(4,128)(2,1)} reshape(bf16[512,1536]{1,0:T(8,128)(2,1)} %convolution_convert_fusion.2) | data formatting | bytes 3145728 | tf_op jit(solution)/shard_map/reshape | solution.py:51
  72.1 2.9 fusion.26
  76.3 2.2 convolution_convert_fusion.4
  83.8 20.7 %all-gather.9.cloned.1.call-done = bf16[512,2048]{1,0:T(8,128)(2,1)} async-done(((bf16[128,2048]{1,0:T(8,128)(2,1)}), bf16[512,2048]{1,0:T(8,128)(2,1)}) %all-gather.9.cloned.1.call-update) | async-done | bytes 2097168 | tf_op jit(solution)/shard_map/all_gather | solution.py:76
  104.5 3.8 %fusion.27 = f32[512,512]{0,1:T(8,128)} fusion(bf16[512,2048]{1,0:T(8,128)(2,1)} %all-gather.9.cloned.1.call-done, bf16[512,2048]{1,0:T(8,128)(2,1)S(1)} %copy-done), kind=kOutput, calls=%fused_computation.62 | convolution fusion | flops 1073741824 | bytes 5242880 | tf_op jit(solution)/shard_map/dot_general | solution.py:77
  108.4 20.9 %all-gather.11.cloned.1.call-done = bf16[32,128,128]{2,1,0:T(8,128)(2,1)} async-done(((bf16[4,128,128]{2,1,0:T(8,128)(2,1)}), bf16[32,128,128]{2,1,0:T(8,128)(2,1)}) %all-gather.11.cloned.1.call-update) | async-done | bytes 1048592 | tf_op jit(solution)/shard_map/all_gather | solution.py:14
  129.2 8.5 %while.30 = (s32[]{:T(128)}, f32[4,128,128]{2,1,0:T(8,128)S(1)}, s32[]{:T(128)}, bf16[8,4,128,128]{3,2,1,0:T(8,128)(2,1)}, s32[]{:T(128)}, /*index=5*/s32[]{:T(128)}) while((s32[]{:T(128)}, f32[4,128,128]{2,1,0:T(8,128)S(1)}, s32[]{:T(128)}, bf16[8,4,128,128]{3,2,1,0:T(8,128)(2,1)}, s32[]{:T(128)}, /*index=5*/s32[]{:T(128)}) %tuple.107), condition=%wide.region_2.3_spmd.clone, body=%wide.region_1.2_spmd.clone.sunk | while | flops 262148 | bytes 655461 | solution.py:23
  137.7 2.4 multiply_reduce_fusion
  151.8 2.6 fusion.3
  154.5 12.4 %all-gather.13.cloned.1.call-done = bf16[32,128,128]{2,1,0:T(8,128)(2,1)} async-done(((bf16[4,128,128]{2,1,0:T(8,128)(2,1)}), bf16[32,128,128]{2,1,0:T(8,128)(2,1)}) %all-gather.13.cloned.1.call-update) | async-done | bytes 1048592 | tf_op jit(solution)/shard_map/all_gather | solution.py:14
  166.8 8.6 %while.31 = (s32[]{:T(128)}, f32[4,128,128]{2,1,0:T(8,128)S(1)}, s32[]{:T(128)}, bf16[8,4,128,128]{3,2,1,0:T(8,128)(2,1)}, s32[]{:T(128)}, /*index=5*/s32[]{:T(128)}, s32[]{:T(128)}, s32[]{:T(128)}) while((s32[]{:T(128)}, f32[4,128,128]{2,1,0:T(8,128)S(1)}, s32[]{:T(128)}, bf16[8,4,128,128]{3,2,1,0:T(8,128)(2,1)}, s32[]{:T(128)}, ...), condition=%wide.region_8.9_spmd.clone, body=%wide.region_7.8_spmd.clone.sunk | while | flops 262152 | bytes 655523 | solution.py:23
  179.5 7.7 %convolution_convert_fusion = bf16[512,2048]{1,0:T(8,128)(2,1)} fusion(bf16[512,1536]{0,1:T(8,128)(2,1)S(1)} %bitcast.84, bf16[2048,1536]{0,1:T(8,128)(2,1)} %bitcast.81), kind=kOutput, calls=%fused_computation.11 | convolution fusion | flops 3222274048 | bytes 9961472 | tf_op jit(solution)/shard_map/dot_general | solution.py:132
  188.3 2.6 convolution_convert_fusion.1
  191.2 8.3 %multiply_convert_fusion = bf16[2048,1536]{0,1:T(8,128)(2,1)} fusion(bf16[512,1536]{0,1:T(8,128)(2,1)} %bitcast.85, bf16[512,2048]{1,0:T(8,128)(2,1)} %all-gather.7.cloned.1.call-done, f32[2048]{0:T(1024)S(1)} %copy-done.19, f32[512]{0:T(512)S(1)} %add_rsqrt_fusion.1), kind=kOutput, calls=%fused_computation.2 | convolution fusion | flops 3231711232 | bytes 9971712 | tf_op jit(solution)/shard_map/dot_general | solution.py:119
  199.4 8.7 %copy.61 = bf16[2048,3,512]{2,0,1:T(8,128)(2,1)} copy(bf16[2048,3,512]{0,2,1:T(8,128)(2,1)} %bitcast.82) | data formatting | bytes 12582912 | tf_op jit(solution)/shard_map/convert_element_type | solution.py:125
  208.1 3.1 reduce-scatter.11.cloned.1.call-done
  213.1 44.2 %reduce-scatter.7.cloned.1.call-done = bf16[128,2048]{1,0:T(8,128)(2,1)} async-done(((bf16[512,2048]{1,0:T(8,128)(2,1)}), bf16[128,2048]{1,0:T(8,128)(2,1)}) %reduce-scatter.7.cloned.1.call-update) | async-done | bytes 524304 | tf_op jit(solution)/shard_map/reduce_scatter | solution.py:131
  258.7 44.1 %reduce-scatter.5.cloned.1.call-done = bf16[128,2048]{1,0:T(8,128)(2,1)} async-done(((bf16[512,2048]{1,0:T(8,128)(2,1)}), bf16[128,2048]{1,0:T(8,128)(2,1)}) %reduce-scatter.5.cloned.1.call-update) | async-done | bytes 524304 | tf_op jit(solution)/shard_map/reduce_scatter | solution.py:68
  302.9 2.7 fusion.15
  305.5 62.2 %reduce-scatter.9.cloned.1.call-done = bf16[256,3,512]{2,0,1:T(8,128)(2,1)} async-done(((bf16[2048,3,512]{2,0,1:T(8,128)(2,1)}), bf16[256,3,512]{2,0,1:T(8,128)(2,1)}) %reduce-scatter.9.cloned.1.call-update) | async-done | bytes 786448 | tf_op jit(solution)/shard_map/reduce_scatter | solution.py:122
  367.8 2.5 convert_element_type.139
  (99 shorter events, 47.3 us)
Async XLA Ops:
  7.2 97.3 %copy-start = (bf16[512,2048]{1,0:T(8,128)(2,1)S(1)}, bf16[512,2048]{1,0:T(8,128)(2,1)}, u32[]{:S(2)}) copy-start(bf16[512,2048]{1,0:T(8,128)(2,1)} %param.14) | copy-start | bytes 6291460
  7.2 51.1 %all-gather.7.cloned.1.call-start = ((), (), s32[]{:S(2)}) async-start(), calls=%async_computation.4 | async-start | bytes 2621440 | tf_op jit(solution)/shard_map/all_gather | solution.py:44
  7.9 96.6 %all-gather.9.cloned.1.call-start = ((), (), s32[]{:S(2)}) async-start(), calls=%async_computation.6 | async-start | bytes 2621440 | tf_op jit(solution)/shard_map/all_gather | solution.py:76
  8.7 120.6 %all-gather.11.cloned.1.call-start = ((), (), s32[]{:S(2)}) async-start(), calls=%async_computation.10 | async-start | bytes 1179648 | tf_op jit(solution)/shard_map/all_gather | solution.py:14
  8.7 51.8 %copy-start.19 = (f32[2048]{0:T(1024)S(1)}, f32[2048]{0:T(1024)}, u32[]{:S(2)}) copy-start(f32[2048]{0:T(1024)} %param.11) | copy-start | bytes 24580
  58.3 2.2 copy-start.12
  76.2 4.4 %copy-start.3 = (bf16[512,1,4,128]{0,3,2,1:T(8,128)(2,1)}, bf16[512,1,4,128]{0,3,2,1:T(8,128)(2,1)S(1)}, u32[]{:S(2)}) copy-start(bf16[512,1,4,128]{0,3,2,1:T(8,128)(2,1)S(1)} %copy.75) | copy-start | bytes 1572868
  78.5 88.3 %all-gather.13.cloned.1.call-start = ((), (), s32[]{:S(2)}) async-start(), calls=%async_computation.11 | async-start | bytes 1179648 | tf_op jit(solution)/shard_map/all_gather | solution.py:14
  78.7 2.0 copy-start.17
  108.4 29.4 %copy-start.20 = (f32[512]{0:T(512)S(1)}, f32[512]{0:T(512)}, u32[]{:S(2)}) copy-start(f32[512]{0:T(512)} %param.13) | copy-start | bytes 6148
  137.7 2.5 copy-start.10
  140.2 3.2 copy-start.18
  143.2 68.0 %reduce-scatter.11.cloned.1.call-start = ((), (), s32[]{:S(2)}) async-start(), calls=%async_computation.9 | async-start | bytes 2359296 | tf_op jit(solution)/shard_map/reduce_scatter | solution.py:90
  143.4 2.1 copy-start.5
  146.6 1.6 copy-start.2
  149.6 2.2 copy-start.21
  154.4 102.9 %reduce-scatter.7.cloned.1.call-start = ((), (), s32[]{:S(2)}) async-start(), calls=%async_computation.7 | async-start | bytes 2621440 | tf_op jit(solution)/shard_map/reduce_scatter | solution.py:131
  166.8 10.7 %copy-start.4 = (bf16[512,1,4,128]{0,3,2,1:T(8,128)(2,1)S(1)}, bf16[512,1,4,128]{0,3,2,1:T(8,128)(2,1)}, u32[]{:S(2)}) copy-start(bf16[512,1,4,128]{0,3,2,1:T(8,128)(2,1)} %copy-done.3) | copy-start | bytes 1572868
  175.4 2.2 copy-start.9
  175.4 2.8 copy-start.13
  187.3 115.6 %reduce-scatter.5.cloned.1.call-start = ((), (), s32[]{:S(2)}) async-start(), calls=%async_computation.5 | async-start | bytes 2621440 | tf_op jit(solution)/shard_map/reduce_scatter | solution.py:68
  190.9 176.9 %reduce-scatter.9.cloned.1.call-start = ((), (), s32[]{:S(2)}) async-start(), calls=%async_computation.8 | async-start | bytes 7077888 | tf_op jit(solution)/shard_map/reduce_scatter | solution.py:122
  208.1 49.3 %copy-start.8 = (bf16[128,2048]{1,0:T(8,128)(2,1)S(1)}, bf16[128,2048]{1,0:T(8,128)(2,1)}, u32[]{:S(2)}) copy-start(bf16[128,2048]{1,0:T(8,128)(2,1)} %param.10) | copy-start | bytes 1572868
  208.1 94.8 %copy-start.11 = (bf16[128,2048]{1,0:T(8,128)(2,1)S(1)}, bf16[128,2048]{1,0:T(8,128)(2,1)}, u32[]{:S(2)}) copy-start(bf16[128,2048]{1,0:T(8,128)(2,1)} %param.15) | copy-start | bytes 1572868
  (6 other events, 6.9 us)
Sparse Core Ops, SparseCore 0:
  9.6 48.6 all-gather.6
  59.8 44.6 all-gather.8
  107.0 22.1 all-gather.10
  143.3 23.4 all-gather.12
  170.0 41.2 reduce-scatter.10
  213.5 43.8 reduce-scatter.6
  259.6 43.1 reduce-scatter.4
  306.6 61.1 reduce-scatter.8
where the time goes:
time: 379 us; the launch traced here: 377 us
  waiting for transfers between devices  250 us (66%)
  matrix products  52 us (14%)
  local copies, waits for them, and re-layouts  33 us (9%)
  other arithmetic  26.8 us (7%)
  between operations  14.5 us (4%)
    reduce_scatter x1, waiting for transfers between devices, shards(): lax.psum_scatter((product * factor).reshape(ctx_rows * lax.axis_size('ctx...  62.2 us
    reduce_scatter x1, waiting for transfers between devices, shards(): lax.psum_scatter(lax.dot_general(rows, flat_weight, (((1,), (1,)), ((), (...  44.2 us
    reduce_scatter x1, waiting for transfers between devices, shards(): lax.psum_scatter(jnp.dot(rows, out_weight, preferred_element_type=jnp.flo...  44.1 us
    all_gather x1, waiting for transfers between devices, shards(): lax.all_gather(inputs, 'tp', axis=0, tiled=True).astype(jnp.float32)  40.7 us
    all_gather x2, waiting for transfers between devices, carried_in(): everything = lax.all_gather(array.astype(jnp.bfloat16), axis)  33.2 us
    all_gather x1, waiting for transfers between devices, shards(): cotangent = lax.all_gather(out_cotangent, 'tp', axis=0, tiled=True)  20.7 us
    unnamed x47, local copies, waits for them, and re-layouts  17.5 us
    select_n x16, other arithmetic, hop(): return jnp.where(reached, new, before)  16.7 us
  transfers between devices with their start and end apart: 8, of which 8 were waited for; matrix products, arithmetic and copies ran while one was open for 24% of the time, Pallas kernels for 0%

commit v1 on v0

--- a/solution.py
+++ b/solution.py
@@ -7,6 +7,22 @@
 DH = 128
 EPSILON = 1e-05
 highest = lax.Precision.HIGHEST
+
+
+def ring_gather(x, axis, dim):
+    ways, here, step = (lax.axis_size(axis), lax.axis_index(axis), x.shape[dim])
+    lengths = [n * ways if d == dim else n for d, n in enumerate(x.shape)]
+    full = lax.dynamic_update_slice_in_dim(jnp.zeros(lengths, x.dtype), x, here * step, axis=dim)
+    going_up = going_down = x
+    for far in range(1, ways // 2 + 1):
+        going_up = lax.ppermute(going_up, axis, [(d, (d + 1) % ways) for d in range(ways)])
+        full = lax.dynamic_update_slice_in_dim(full, going_up, (here - far) % ways * step, axis=dim)
+        if 2 * far < ways:
+            going_down = lax.ppermute(going_down, axis, [(d, (d - 1) % ways) for d in range(ways)])
+            full = lax.dynamic_update_slice_in_dim(
+                full, going_down, (here + far) % ways * step, axis=dim
+            )
+    return full
 
 
 def carried_in(array, axis, combine, identity, reverse):
@@ -73,7 +89,7 @@
     ).astype(jnp.float32)
     inputs_f = inputs.astype(jnp.float32)
     outputs = (inputs_f + attn_sum).astype(jnp.bfloat16)
-    cotangent = lax.all_gather(out_cotangent, "tp", axis=0, tiled=True)
+    cotangent = ring_gather(out_cotangent, "tp", 0)
     grad_mixed = lax.dot_general(
         cotangent, out_weight, (((1,), (1,)), ((), ())), preferred_element_type=jnp.float32
     ).reshape(block, heads, DH)

time: 379 us -> 374 us (0.987)
  waiting for transfers between devices: 250 us -> 226 us
  starting transfers between devices: 0.72 us -> 11.5 us
  local copies, waits for them, and re-layouts: 33 us -> 37.9 us
    all_gather x1 -> x0, waiting for transfers between devices: 20.7 us -> none  [shards(): cotangent = lax.all_gather(out_cotangent, 'tp', axis=0, tiled=True)]
    all_gather x2, waiting for transfers between devices: 33.2 us -> 19.8 us  [carried_in(): everything = lax.all_gather(array.astype(jnp.bfloat16), axis)]
    ppermute x0 -> x3, starting transfers between devices: none -> 10.8 us  [the longest x2 8.68 us: ring_gather(): lax.ppermute(going_up, axis, [(d, (d + 1) % ways) for d in range(ways)])]
    all_gather x1, waiting for transfers between devices: 40.7 us -> 48.6 us  [shards(): lax.all_gather(inputs, 'tp', axis=0, tiled=True).astype(jnp.float32)]
    dynamic_update_slice x0 -> x4, local copies, waits for them, and re-layouts: none -> 6.57 us  [the longest x2 3.79 us: ring_gather(): lax.dynamic_update_slice_in_dim(full, going_up, (here - far) % ways * ste...]
    unnamed x47 -> x48, local copies, waits for them, and re-layouts: 17.5 us -> 14.2 us
  transfers between devices with their start and end apart: 8 -> 10, of which waited for: 8 -> 8; matrix products, arithmetic and copies ran while one was open for 24% -> 27% of each run, Pallas kernels for 0% -> 0%
where the time goes in v1:
time: 374 us; the launch traced here: 372 us
  waiting for transfers between devices  226 us (60%)
  matrix products  52.5 us (14%)
  local copies, waits for them, and re-layouts  37.9 us (10%)
  other arithmetic  29.4 us (8%)
  between operations  14.4 us (4%)
  starting transfers between devices  11.5 us (3%)
    reduce_scatter x1, waiting for transfers between devices, shards(): lax.psum_scatter((product * factor).reshape(ctx_rows * lax.axis_size('ctx...  62.2 us
    all_gather x1, waiting for transfers between devices, shards(): lax.all_gather(inputs, 'tp', axis=0, tiled=True).astype(jnp.float32)  48.6 us
    reduce_scatter x1, waiting for transfers between devices, shards(): lax.psum_scatter(lax.dot_general(rows, flat_weight, (((1,), (1,)), ((), (...  44.3 us
    reduce_scatter x1, waiting for transfers between devices, shards(): lax.psum_scatter(jnp.dot(rows, out_weight, preferred_element_type=jnp.flo...  44 us
    all_gather x2, waiting for transfers between devices, carried_in(): everything = lax.all_gather(array.astype(jnp.bfloat16), axis)  19.8 us
    select_n x16, other arithmetic, hop(): return jnp.where(reached, new, before)  16.7 us
    unnamed x48, local copies, waits for them, and re-layouts  14.2 us
    ppermute x2, starting transfers between devices, ring_gather(): lax.ppermute(going_up, axis, [(d, (d + 1) % ways) for d in range(ways)])  8.68 us
  transfers between devices with their start and end apart: 10, of which 8 were waited for; matrix products, arithmetic and copies ran while one was open for 27% of the time, Pallas kernels for 0%

profile of v1, /device:TPU:0, one launch (start us, length us, event | category | flops | bytes accessed | tf_op | source)
XLA Modules:
  0.0 372.0 jit_solution(8122877512697547511)
XLA Ops:
  8.0 3.1 collective-permute-start
  13.1 9.0 %copy.43 = bf16[2048,3,512]{0,2,1:T(8,128)(2,1)} copy(bf16[2048,3,512]{2,0,1:T(8,128)(2,1)} %param.12) | data formatting | bytes 12582912 | tf_op args[2]
  24.6 2.9 collective-permute-done
  27.6 5.6 %collective-permute-start.2 = (bf16[128,2048]{1,0:T(8,128)(2,1)}, bf16[128,2048]{1,0:T(8,128)(2,1)}, u32[]{:S(2)}, u32[]{:S(2)}) collective-permute-start(bf16[128,2048]{1,0:T(8,128)(2,1)} %collective-permute-done), channel_id=1, source_target_pairs={{0,1},{1,2},{2,3},{3,0},{4,5},{5,6},{6,7},{7,4},{8,9},{9,10},{10,1... | collective-permute-start | bytes 1572872 | tf_op jit(solution)/shard_map/ppermute | solution.py:18
  33.2 48.6 %all-gather.6.cloned.1.call-done = bf16[512,2048]{1,0:T(8,128)(2,1)} async-done(((bf16[128,2048]{1,0:T(8,128)(2,1)}), bf16[512,2048]{1,0:T(8,128)(2,1)}) %all-gather.6.cloned.1.call-update) | async-done | bytes 2097168 | tf_op jit(solution)/shard_map/all_gather | solution.py:60
  84.1 7.6 %convolution_convert_fusion.2 = bf16[512,1536]{1,0:T(8,128)(2,1)} fusion(bf16[2048,1536]{0,1:T(8,128)(2,1)} %bitcast.78, bf16[512,2048]{1,0:T(8,128)(2,1)S(1)} %copy-done.13, f32[2048]{0:T(1024)S(1)} %copy-done.21, f32[512]{0:T(512)S(1)} %add_rsqrt_fusion.1), kind=kOutput, calls=%fused_computation.13 | convolution fusion | flops 3226206208 | bytes 9971712 | tf_op jit(solution)/shard_map/dot_general | solution.py:62
  91.7 3.9 %reshape.88 = bf16[512,3,4,128]{3,2,1,0:T(4,128)(2,1)} reshape(bf16[512,1536]{1,0:T(8,128)(2,1)} %convolution_convert_fusion.2) | data formatting | bytes 3145728 | tf_op jit(solution)/shard_map/reshape | solution.py:67
  95.6 2.9 fusion.25
  108.6 4.0 %fusion.26 = f32[512,512]{0,1:T(8,128)} fusion(bf16[512,2048]{1,0:T(8,128)(2,1)} %constant_dynamic-update-slice_fusion, bf16[512,2048]{1,0:T(8,128)(2,1)S(1)} %copy-done), kind=kOutput, calls=%fused_computation.65 | convolution fusion | flops 1073741824 | bytes 5242880 | tf_op jit(solution)/shard_map/dot_general | solution.py:93
  116.6 8.5 %all-gather.8.cloned.1.call-done = bf16[32,128,128]{2,1,0:T(8,128)(2,1)} async-done(((bf16[4,128,128]{2,1,0:T(8,128)(2,1)}), bf16[32,128,128]{2,1,0:T(8,128)(2,1)}) %all-gather.8.cloned.1.call-update) | async-done | bytes 1048592 | tf_op jit(solution)/shard_map/all_gather | solution.py:30
  125.1 8.5 %while.30 = (s32[]{:T(128)}, f32[4,128,128]{2,1,0:T(8,128)S(1)}, s32[]{:T(128)}, bf16[8,4,128,128]{3,2,1,0:T(8,128)(2,1)}, s32[]{:T(128)}, /*index=5*/s32[]{:T(128)}) while((s32[]{:T(128)}, f32[4,128,128]{2,1,0:T(8,128)S(1)}, s32[]{:T(128)}, bf16[8,4,128,128]{3,2,1,0:T(8,128)(2,1)}, s32[]{:T(128)}, /*index=5*/s32[]{:T(128)}) %tuple.101), condition=%wide.region_2.3_spmd.clone, body=%wide.region_1.2_spmd.clone.sunk | while | flops 262148 | bytes 655461 | solution.py:39
  146.2 4.2 %multiply_convert_fusion.1 = bf16[2048,512]{1,0:T(8,128)(2,1)} fusion(bf16[512,2048]{1,0:T(8,128)(2,1)} %constant_dynamic-update-slice_fusion, bf16[512,512]{0,1:T(8,128)(2,1)S(1)} %bitcast.84), kind=kOutput, calls=%fused_computation.8 | convolution fusion | flops 1075838976 | bytes 4718592 | tf_op jit(solution)/shard_map/dot_general | solution.py:108
  150.5 11.4 %all-gather.10.cloned.1.call-done = bf16[32,128,128]{2,1,0:T(8,128)(2,1)} async-done(((bf16[4,128,128]{2,1,0:T(8,128)(2,1)}), bf16[32,128,128]{2,1,0:T(8,128)(2,1)}) %all-gather.10.cloned.1.call-update) | async-done | bytes 1048592 | tf_op jit(solution)/shard_map/all_gather | solution.py:30
  161.9 8.6 %while.31 = (s32[]{:T(128)}, f32[4,128,128]{2,1,0:T(8,128)S(1)}, s32[]{:T(128)}, bf16[8,4,128,128]{3,2,1,0:T(8,128)(2,1)}, s32[]{:T(128)}, /*index=5*/s32[]{:T(128)}, s32[]{:T(128)}, s32[]{:T(128)}) while((s32[]{:T(128)}, f32[4,128,128]{2,1,0:T(8,128)S(1)}, s32[]{:T(128)}, bf16[8,4,128,128]{3,2,1,0:T(8,128)(2,1)}, s32[]{:T(128)}, ...), condition=%wide.region_8.9_spmd.clone, body=%wide.region_7.8_spmd.clone.sunk | while | flops 262152 | bytes 655523 | solution.py:39
  174.4 7.7 %convolution_convert_fusion = bf16[512,2048]{1,0:T(8,128)(2,1)} fusion(bf16[512,1536]{0,1:T(8,128)(2,1)S(1)} %bitcast.82, bf16[2048,1536]{0,1:T(8,128)(2,1)} %bitcast.79), kind=kOutput, calls=%fused_computation.11 | convolution fusion | flops 3222274048 | bytes 9961472 | tf_op jit(solution)/shard_map/dot_general | solution.py:148
  183.2 2.6 convolution_convert_fusion.1
  186.0 8.3 %multiply_convert_fusion = bf16[2048,1536]{0,1:T(8,128)(2,1)} fusion(bf16[512,1536]{0,1:T(8,128)(2,1)} %bitcast.83, bf16[512,2048]{1,0:T(8,128)(2,1)} %all-gather.6.cloned.1.call-done, f32[2048]{0:T(1024)S(1)} %copy-done.21, f32[512]{0:T(512)S(1)} %add_rsqrt_fusion.1), kind=kOutput, calls=%fused_computation.2 | convolution fusion | flops 3231711232 | bytes 9971712 | tf_op jit(solution)/shard_map/dot_general | solution.py:135
  194.3 8.6 %copy.59 = bf16[2048,3,512]{2,0,1:T(8,128)(2,1)} copy(bf16[2048,3,512]{0,2,1:T(8,128)(2,1)} %bitcast.80) | data formatting | bytes 12582912 | tf_op jit(solution)/shard_map/convert_element_type | solution.py:141
  203.0 3.3 reduce-scatter.11.cloned.1.call-done
  208.1 44.3 %reduce-scatter.7.cloned.1.call-done = bf16[128,2048]{1,0:T(8,128)(2,1)} async-done(((bf16[512,2048]{1,0:T(8,128)(2,1)}), bf16[128,2048]{1,0:T(8,128)(2,1)}) %reduce-scatter.7.cloned.1.call-update) | async-done | bytes 524304 | tf_op jit(solution)/shard_map/reduce_scatter | solution.py:147
  253.8 44.0 %reduce-scatter.5.cloned.1.call-done = bf16[128,2048]{1,0:T(8,128)(2,1)} async-done(((bf16[512,2048]{1,0:T(8,128)(2,1)}), bf16[128,2048]{1,0:T(8,128)(2,1)}) %reduce-scatter.5.cloned.1.call-update) | async-done | bytes 524304 | tf_op jit(solution)/shard_map/reduce_scatter | solution.py:84
  297.8 2.7 fusion.14
  300.4 62.2 %reduce-scatter.9.cloned.1.call-done = bf16[256,3,512]{2,0,1:T(8,128)(2,1)} async-done(((bf16[2048,3,512]{2,0,1:T(8,128)(2,1)}), bf16[256,3,512]{2,0,1:T(8,128)(2,1)}) %reduce-scatter.9.cloned.1.call-update) | async-done | bytes 786448 | tf_op jit(solution)/shard_map/reduce_scatter | solution.py:138
  362.7 2.5 convert_element_type.136
  (109 shorter events, 59.4 us)
Async XLA Ops:
  7.2 101.4 %copy-start = (bf16[512,2048]{1,0:T(8,128)(2,1)S(1)}, bf16[512,2048]{1,0:T(8,128)(2,1)}, u32[]{:S(2)}) copy-start(bf16[512,2048]{1,0:T(8,128)(2,1)} %param.14) | copy-start | bytes 6291460
  7.2 74.6 %all-gather.6.cloned.1.call-start = ((), (), s32[]{:S(2)}) async-start(), calls=%async_computation.4 | async-start | bytes 2621440 | tf_op jit(solution)/shard_map/all_gather | solution.py:60
  7.9 117.2 %all-gather.8.cloned.1.call-start = ((), (), s32[]{:S(2)}) async-start(), calls=%async_computation.9 | async-start | bytes 1179648 | tf_op jit(solution)/shard_map/all_gather | solution.py:30
  8.0 19.6 %collective-permute-start = (bf16[128,2048]{1,0:T(8,128)(2,1)}, bf16[128,2048]{1,0:T(8,128)(2,1)}, u32[]{:S(2)}, u32[]{:S(2)}) collective-permute-start(bf16[128,2048]{1,0:T(8,128)(2,1)} %param.15), channel_id=1, source_target_pairs={{0,1},{1,2},{2,3},{3,0},{4,5},{5,6},{6,7},{7,4},{8,9},{9,10},{10,1... | collective-permute-start | bytes 1572872 | tf_op jit(solution)/shard_map/ppermute | solution.py:18
  11.0 93.8 %collective-permute-start.1 = (bf16[128,2048]{1,0:T(8,128)(2,1)}, bf16[128,2048]{1,0:T(8,128)(2,1)}, u32[]{:S(2)}, u32[]{:S(2)}) collective-permute-start(bf16[128,2048]{1,0:T(8,128)(2,1)} %param.15), channel_id=1, source_target_pairs={{0,3},{1,0},{2,1},{3,2},{4,7},{5,4},{6,5},{7,6},{8,11},{9,8},{10,9... | collective-permute-start | bytes 1572872 | tf_op jit(solution)/shard_map/ppermute | solution.py:21
  23.7 60.3 %copy-start.21 = (f32[2048]{0:T(1024)S(1)}, f32[2048]{0:T(1024)}, u32[]{:S(2)}) copy-start(f32[2048]{0:T(1024)} %param.11) | copy-start | bytes 24580
  27.6 79.2 %collective-permute-start.2 = (bf16[128,2048]{1,0:T(8,128)(2,1)}, bf16[128,2048]{1,0:T(8,128)(2,1)}, u32[]{:S(2)}, u32[]{:S(2)}) collective-permute-start(bf16[128,2048]{1,0:T(8,128)(2,1)} %collective-permute-done), channel_id=1, source_target_pairs={{0,1},{1,2},{2,3},{3,0},{4,5},{5,6},{6,7},{7,4},{8,9},{9,10},{10,1... | collective-permute-start | bytes 1572872 | tf_op jit(solution)/shard_map/ppermute | solution.py:18
  81.8 2.2 copy-start.13
  99.8 13.6 %copy-start.3 = (bf16[512,1,4,128]{0,3,2,1:T(8,128)(2,1)}, bf16[512,1,4,128]{0,3,2,1:T(8,128)(2,1)S(1)}, u32[]{:S(2)}) copy-start(bf16[512,1,4,128]{0,3,2,1:T(8,128)(2,1)S(1)} %copy.72) | copy-start | bytes 1572868
  102.1 59.8 %all-gather.10.cloned.1.call-start = ((), (), s32[]{:S(2)}) async-start(), calls=%async_computation.10 | async-start | bytes 1179648 | tf_op jit(solution)/shard_map/all_gather | solution.py:30
  108.6 4.0 %copy-start.5 = (bf16[512,1,4,128]{3,2,1,0:T(4,128)(2,1)S(1)}, bf16[512,1,4,128]{3,2,1,0:T(4,128)(2,1)}, u32[]{:S(2)}) copy-start(bf16[512,1,4,128]{3,2,1,0:T(4,128)(2,1)} %get-tuple-element.246) | copy-start | bytes 1572868
  108.6 4.0 %copy-start.20 = (pred[512,512]{1,0:T(8,128)(4,1)S(1)}, pred[512,512]{1,0:T(8,128)(4,1)}, u32[]{:S(2)}) copy-start(pred[512,512]{1,0:T(8,128)(4,1)} %iota_compare_fusion) | copy-start | bytes 786436
  116.6 17.0 %copy-start.22 = (f32[512]{0:T(512)S(1)}, f32[512]{0:T(512)}, u32[]{:S(2)}) copy-start(f32[512]{0:T(512)} %param.13) | copy-start | bytes 6148
  133.5 2.5 copy-start.12
  138.2 68.0 %reduce-scatter.11.cloned.1.call-start = ((), (), s32[]{:S(2)}) async-start(), calls=%async_computation.8 | async-start | bytes 2359296 | tf_op jit(solution)/shard_map/reduce_scatter | solution.py:106
  138.5 2.2 copy-start.6
  150.5 20.0 %copy-start.7 = (bf16[512,1,4,128]{3,2,1,0:T(4,128)(2,1)S(1)}, bf16[512,1,4,128]{3,2,1,0:T(4,128)(2,1)}, u32[]{:S(2)}) copy-start(bf16[512,1,4,128]{3,2,1,0:T(4,128)(2,1)} %get-tuple-element.246) | copy-start | bytes 1572868
  150.5 101.9 %reduce-scatter.7.cloned.1.call-start = ((), (), s32[]{:S(2)}) async-start(), calls=%async_computation.6 | async-start | bytes 2621440 | tf_op jit(solution)/shard_map/reduce_scatter | solution.py:147
  161.9 10.6 %copy-start.4 = (bf16[512,1,4,128]{0,3,2,1:T(8,128)(2,1)S(1)}, bf16[512,1,4,128]{0,3,2,1:T(8,128)(2,1)}, u32[]{:S(2)}) copy-start(bf16[512,1,4,128]{0,3,2,1:T(8,128)(2,1)} %copy-done.3) | copy-start | bytes 1572868
  170.5 2.6 copy-start.16
  182.2 115.6 %reduce-scatter.5.cloned.1.call-start = ((), (), s32[]{:S(2)}) async-start(), calls=%async_computation.5 | async-start | bytes 2621440 | tf_op jit(solution)/shard_map/reduce_scatter | solution.py:84
  185.8 176.9 %reduce-scatter.9.cloned.1.call-start = ((), (), s32[]{:S(2)}) async-start(), calls=%async_computation.7 | async-start | bytes 7077888 | tf_op jit(solution)/shard_map/reduce_scatter | solution.py:138
  203.0 49.4 %copy-start.10 = (bf16[128,2048]{1,0:T(8,128)(2,1)S(1)}, bf16[128,2048]{1,0:T(8,128)(2,1)}, u32[]{:S(2)}) copy-start(bf16[128,2048]{1,0:T(8,128)(2,1)} %param.10) | copy-start | bytes 1572868
  203.0 94.8 %copy-start.15 = (bf16[128,2048]{1,0:T(8,128)(2,1)S(1)}, bf16[128,2048]{1,0:T(8,128)(2,1)}, u32[]{:S(2)}) copy-start(bf16[128,2048]{1,0:T(8,128)(2,1)} %param.15) | copy-start | bytes 1572868
  (9 other events, 12.6 us)
Sparse Core Ops, SparseCore 0:
  9.6 72.1 all-gather.5
  102.2 22.8 all-gather.7
  138.4 23.4 all-gather.9
  165.0 41.1 reduce-scatter.10
  208.5 43.8 reduce-scatter.6
  254.5 43.1 reduce-scatter.4
  301.5 61.1 reduce-scatter.8
